TPU v7x, 32 devices: a whole 2x2x4 slice. The times are simulated.
32 devices in a mesh: grid: 8 (over z, y), vec: 4 (over x, core).
Axes of the slice: x: 2, y: 2, z: 4, core: 2. Of those that a mesh axis runs over, the one named last changes fastest.
Arguments:
- trial_block: float32 [16, 48, 32, 128], P('vec', 'grid'), may hold values from -60 to 60, as said below
- response_weight: float32 [48, 32, 128], P('grid'), may hold values from 2 to 5
Outputs:
- rotated: float32 [16, 48, 32, 128], P('vec', 'grid')
- potentials: float32 [16, 48, 32, 128], P('vec', 'grid')
- ritz_matrix: float32 [16, 16], replicated
Inputs may be any that keep to these rules, and one draw needn't show every extreme that they name: `trial_block`: trial vectors whose Gram matrix is positive definite.
All inputs are finite; a program needn't handle non-finite values.
Results may differ from a plain program's by a relative error of at most 0.0002.
Values sent between devices are 32-bit elements; how exact they have to be, the bound alone decides.
A program may use at most 64 MiB of HBM per device.

v0:
```python
import functools

import jax
import jax.numpy as jnp
from jax import lax
from jax.experimental import pallas as pl
from jax.experimental.pallas import tpu as pltpu
from jax.sharding import PartitionSpec as P

ITERS = 3


COEFFS = (
    -5369.0 / 1800.0,
    12.0 / 7.0,
    -15.0 / 56.0,
    10.0 / 189.0,
    -1.0 / 112.0,
    2.0 / 1925.0,
    -1.0 / 16632.0,
)


def shifted(value, axis, steps):
    count = lax.axis_size(axis)
    pairs = [(source, (source + steps) % count) for source in range(count)]
    return lax.ppermute(value, axis, pairs)


def with_halo(cells, sides, width):
    for axis, dim in sides:
        count = lax.axis_size(axis)
        head = lax.slice_in_dim(cells, 0, width, axis=dim)
        tail = lax.slice_in_dim(cells, cells.shape[dim] - width, cells.shape[dim], axis=dim)
        cells = jnp.concatenate(
            [
                lax.ppermute(tail, axis, [(i, (i + 1) % count) for i in range(count)]),
                cells,
                lax.ppermute(head, axis, [((i + 1) % count, i) for i in range(count)]),
            ],
            axis=dim,
        )
    return cells


def along_axis(total, padded, axis, length):
    for offset in range(1, 7):
        upper = lax.slice_in_dim(padded, 6 + offset, 6 + offset + length, axis=axis)
        lower = lax.slice_in_dim(padded, 6 - offset, 6 - offset + length, axis=axis)
        total = total + COEFFS[offset] * (upper + lower)
    return total


def operate(field):
    stride = max(lax.axis_size("grid") // 16, 2)
    row_count = field.shape[1]
    col_count = field.shape[2]
    total = 3.0 * COEFFS[0] * field
    below = shifted(field, "grid", stride)
    above = shifted(field, "grid", -stride)
    along_x = jnp.concatenate([below, field, above], axis=1)
    total = along_axis(total, along_x, 1, row_count)
    side_halo = with_halo(field, (("grid", 2),), 6)
    total = along_axis(total, side_halo, 2, col_count)
    along_z = jnp.pad(field, ((0, 0), (0, 0), (0, 0), (6, 6)))
    total = along_axis(total, along_z, 3, field.shape[3])
    return -total


def inner(left, right):
    return jnp.sum(left * right, axis=(1, 2, 3))


def expand(values):
    return values[:, None, None, None]


def two_products(residual, image):
    return lax.psum((inner(residual, residual), inner(residual, image)), "grid")


def finish(gram, cross, cells):
    high = lax.Precision.HIGHEST
    gram = gram / cells
    cross = cross / cells
    lower = jnp.linalg.cholesky(gram)
    inverse = lax.linalg.triangular_solve(
        lower, jnp.eye(gram.shape[0], dtype=jnp.float32), left_side=True, lower=True
    )
    middle = jnp.dot(inverse, 0.5 * (cross + cross.T), precision=high)
    return (inverse, jnp.dot(middle, inverse.T, precision=high))


def body(trial_block, response_weight):
    high = lax.Precision.HIGHEST
    source = response_weight[None] * trial_block
    solution = jnp.zeros_like(source)
    residual = source
    image = operate(residual)
    norm_now, product = two_products(residual, image)
    alpha = norm_now / product
    direction, along = (residual, image)
    for step in range(ITERS):
        solution = solution + expand(alpha) * direction
        residual = residual - expand(alpha) * along
        if step + 1 < ITERS:
            image = operate(residual)
            norm_next, product = two_products(residual, image)
            ratio = norm_next / norm_now
            alpha = norm_next / (product - ratio * norm_next / alpha)
            direction = residual + expand(ratio) * direction
            along = image + expand(ratio) * along
            norm_now = norm_next
    local_count = trial_block.shape[0]
    whole_x, whole_p = (
        lax.all_gather(trial_block, "vec", axis=0, tiled=True),
        lax.all_gather(solution, "vec", axis=0, tiled=True),
    )
    flat_x = whole_x.reshape(whole_x.shape[0], -1)
    flat_p = whole_p.reshape(whole_p.shape[0], -1)
    gram, cross = lax.psum(
        (jnp.dot(flat_x, flat_x.T, precision=high), jnp.dot(flat_x, flat_p.T, precision=high)),
        "grid",
    )
    cells = lax.axis_size("grid") * flat_x.shape[1]
    inverse, ritz_matrix = finish(gram, cross, cells)
    own_rows = lax.dynamic_slice_in_dim(
        inverse, lax.axis_index("vec") * local_count, local_count, 0
    )
    rotated = jnp.dot(own_rows, flat_x, precision=high).reshape(trial_block.shape)
    potentials = jnp.dot(own_rows, flat_p, precision=high).reshape(trial_block.shape)
    return (rotated, potentials, ritz_matrix)


MESH_ID = pl.DeviceIdType.MESH
PAD = 8
HALO = 6


def kernel(
    groups, parts, trial, weight, rotated, potentials, ritz,
    wbuf, src, pad, img, dirn, along, phi, sums, sums_in, held, waves, gmsg, gin, cmsg, cin, mats, coef,
    fsend, frecv, hsend, hrecv, ssend, srecv, tsend, trecv, rsend, rrecv,
    bsend, brecv, psend, precv, xsend, xrecv, ysend, yrecv, gsend, grecv, csend, crecv, isend,
):
    nl, rows, cols, depth = trial.shape
    nvec = parts * nl
    length = pad.shape[0]
    blocks = length // rows
    pairs = parts // 2
    total_devices = groups * parts
    me_g = lax.axis_index("grid")
    me_v = lax.axis_index("vec")
    me = me_g * parts + me_v
    pair = lax.div(me_v, 2)
    core = lax.rem(me_v, 2)
    partner = (me_g, pair * 2 + 1 - core)
    blk = lax.div(me_g, 2)
    half = lax.rem(me_g, 2)
    center = slice(PAD, PAD + cols)

    barrier = pltpu.get_barrier_semaphore()

    def device_at(k):
        target = lax.rem(me + k, total_devices)
        return (lax.div(target, parts), lax.rem(target, parts))

    def greet(k, carry):
        pl.semaphore_signal(barrier, inc=1, device_id=device_at(k), device_id_type=MESH_ID)
        return carry

    lax.fori_loop(1, total_devices, greet, 0)

    fetches = [
        pltpu.make_async_copy(weight, wbuf, isend.at[0]),
        pltpu.make_async_copy(trial, held.at[pl.ds(me_v * nl, nl)], isend.at[1]),
    ]
    for fetch in fetches:
        fetch.start()
    for fetch in fetches:
        fetch.wait()

    def prepare(i, carry):
        scale = wbuf[i]
        for s in range(nl):
            src[s, i] = scale * held[me_v * nl + s, i]
        return carry

    lax.fori_loop(0, rows, prepare, 0)
    pl.semaphore_wait(barrier, total_devices - 1)

    def remote(source, target, send, recv, device):
        return pltpu.make_async_remote_copy(
            src_ref=source, dst_ref=target, send_sem=send, recv_sem=recv,
            device_id=device, device_id_type=MESH_ID,
        )

    def forward(s):
        return remote(
            src.at[s], pad.at[pl.ds(blk * rows, rows), center], fsend.at[s], frecv.at[blk],
            (core * nl + s, pair * 2 + half),
        )

    def own_slot(s):
        return jnp.logical_and(core * nl + s == me_g, half == core)

    for step in range(nl):
        s = lax.rem(me_g + step, nl)

        @pl.when(jnp.logical_not(own_slot(s)))
        def _():
            forward(s).start()

        @pl.when(own_slot(s))
        def _():
            pad[pl.ds(blk * rows, rows), center] = src[s]

    def slot_ref(buffer, v):
        return buffer.at[pl.ds(v * nl, nl)]

    def trial_copy(q):
        device = partner if q == 0 else (me_g, lax.rem(pair + q, pairs) * 2 + core)
        return remote(slot_ref(held, me_v), slot_ref(held, me_v), tsend.at[q], trecv.at[q], device)

    def from_pair(q):
        return lax.rem(pair - q + pairs, pairs) * 2 + core

    def trial_relay(q):
        v = from_pair(q)
        return remote(slot_ref(held, v), slot_ref(held, v), rsend.at[q], rrecv.at[q], partner)

    for q in list(range(1, pairs)) + [0]:
        trial_copy(q).start()

    def halo(side, bx):
        if side == 0:
            shift, here, there = core, slice(cols, PAD + cols), slice(0, PAD)
        else:
            shift, here, there = core - 1, slice(PAD, 2 * PAD), slice(PAD + cols, 2 * PAD + cols)
        target = lax.rem(bx + shift + blocks, blocks)
        return remote(
            pad.at[pl.ds(bx * rows, rows), here], pad.at[pl.ds(target * rows, rows), there],
            hsend.at[side, bx], hrecv.at[side, bx], partner,
        )

    owner_v = pair * 2 + lax.div(me_g, nl)
    for bx in range(blocks):
        @pl.when(jnp.logical_not(jnp.logical_and(bx * 2 + core == me_g, owner_v == me_v)))
        def _():
            remote(
                src.at[0], pad.at[pl.ds(bx * rows, rows), center], fsend.at[0], frecv.at[bx], partner
            ).wait_recv()

        for side in range(2):
            halo(side, bx).start()

    lane = lax.broadcasted_iota(jnp.int32, (cols, depth), 1)

    halos = [(side, bx) for bx in range(blocks) for side in range(2)]

    def pass_xz(x, carry):
        value = pad[x, center]
        acc = (3.0 * COEFFS[0]) * value
        for k in range(1, HALO + 1):
            near = pad[lax.rem(x + k, length), center] + pad[lax.rem(x + length - k, length), center]
            up = jnp.where(lane < depth - k, pltpu.roll(value, depth - k, 1), 0.0)
            low = jnp.where(lane >= k, pltpu.roll(value, k, 1), 0.0)
            acc = acc + COEFFS[k] * (near + (up + low))
        img[x] = acc
        return carry

    def pass_y(x, carry):
        norm, product = carry
        acc = img[x]
        for k in range(1, HALO + 1):
            acc = acc + COEFFS[k] * (
                pad[x, PAD + k : PAD + k + cols] + pad[x, PAD - k : PAD - k + cols]
            )
        acc = -acc
        img[x] = acc
        value = pad[x, center]
        return (norm + value * value, product + value * acc)

    def folded(value):
        return value.reshape(cols // 8, 8, depth).sum(axis=0)

    def back(bx):
        return remote(
            phi.at[pl.ds(bx * rows, rows)], waves.at[pair * 2 * nl + me_g],
            bsend.at[bx], brecv.at[lax.rem(me_g, nl)], (bx * 2 + core, owner_v),
        )

    lane_row = lax.broadcasted_iota(jnp.int32, (nl, depth), 1)

    def products(buffer, slots):
        def one(j, acc):
            other = held[j]
            parts_of = [
                jnp.sum(jnp.sum(buffer[me_v * nl + s] * other, axis=0), axis=0, keepdims=True)
                for s in slots
            ]
            value = jnp.sum(jnp.concatenate(parts_of, axis=0), axis=1, keepdims=True)
            return jnp.where(lane_row[: len(slots)] == j, value, acc)

        return lax.fori_loop(0, nvec, one, jnp.zeros((len(slots), depth), jnp.float32), unroll=4)

    def spread(message, inbox, send, recv):
        inbox[me_g, me_v] = message[...]

        def start(k, carry):
            remote(message, inbox.at[me_g, me_v], send.at[k], recv.at[me], device_at(k)).start()
            return carry

        lax.fori_loop(1, total_devices, start, 0)

    def collect(message, inbox, send, recv, slot):
        def wait(k, carry):
            g, v = device_at(k)
            copy = remote(message, inbox.at[g, v], send.at[k], recv.at[g * parts + v], (g, v))
            copy.wait_recv()
            copy.wait_send()
            return carry

        lax.fori_loop(1, total_devices, wait, 0)
        for v in range(parts):
            total = inbox[0, v]
            for g in range(1, groups):
                total = total + inbox[g, v]
            mats[slot, v * nl : (v + 1) * nl] = total / (groups * rows * cols * depth)

    norm_now = alpha = None
    for step in range(ITERS):
        lax.fori_loop(0, length, pass_xz, 0, unroll=4)
        for side, bx in halos:
            halo(side, bx).wait_recv()
        zero = jnp.zeros((cols, depth), jnp.float32)
        norm, product = lax.fori_loop(0, length, pass_y, (zero, zero), unroll=4)
        sums[step, 0] = folded(norm)
        sums[step, 1] = folded(product)
        exchange = remote(sums.at[step], sums_in.at[step], ssend.at[step], srecv.at[step], partner)
        exchange.start()
        for side, bx in halos:
            halo(side, bx).wait_send()
        if step == 0:
            for q in range(1, pairs):
                trial_copy(q).wait_recv()
                trial_relay(q).start()
        if step == 1:
            trial_copy(0).wait_recv()
            for q in range(1, pairs):
                trial_relay(q).wait_recv()
            gmsg[...] = products(held, range(nl))
            spread(gmsg, gin, gsend, grecv)
        exchange.wait()
        norm_next = jnp.sum(sums[step, 0] + sums_in[step, 0], axis=(0, 1), keepdims=True)
        product = jnp.sum(sums[step, 1] + sums_in[step, 1], axis=(0, 1), keepdims=True)
        last = step + 1 == ITERS
        if step == 0:
            alpha = norm_next / product
            ratio = None
        else:
            ratio = norm_next / norm_now
            alpha = norm_next / (product - ratio * norm_next / alpha)
            ratio_wide = jnp.broadcast_to(ratio, (cols, depth))
        norm_now = norm_next
        alpha_wide = jnp.broadcast_to(alpha, (cols, depth))

        def update(x, carry):
            value = pad[x, center]
            image = img[x]
            if step == 0:
                phi[x] = alpha_wide * value
                dirn[x] = value
                along[x] = image
            else:
                value_dir = value + ratio_wide * dirn[x]
                phi[x] = phi[x] + alpha_wide * value_dir
                if not last:
                    dirn[x] = value_dir
                    image = image + ratio_wide * along[x]
                    along[x] = image
            if not last:
                pad[x, center] = value - alpha_wide * image
            return carry

        if not last:
            for bx in range(blocks):
                lax.fori_loop(bx * rows, (bx + 1) * rows, update, 0, unroll=rows)
                for side in range(2):
                    halo(side, bx).start()
        else:
            for bx in range(blocks):
                lax.fori_loop(
                    0, rows, lambda i, carry: update(bx * rows + i, carry), 0, unroll=rows
                )
                own = jnp.logical_and(bx * 2 + core == me_g, owner_v == me_v)

                @pl.when(jnp.logical_not(own))
                def _():
                    back(bx).start()

                @pl.when(own)
                def _():
                    waves[pair * 2 * nl + me_g] = phi[pl.ds(bx * rows, rows)]

    def wave_core(s):
        slot = waves.at[me_v * nl + s]
        return remote(slot, slot, psend.at[s], precv.at[s], partner)

    def wave_over(q, s):
        slot = waves.at[me_v * nl + s]
        return remote(
            slot, slot, xsend.at[q, s], xrecv.at[q, s], (me_g, lax.rem(pair + q, pairs) * 2 + core)
        )

    def wave_from(q, s):
        slot = waves.at[from_pair(q) * nl + s]
        return remote(slot, slot, xsend.at[q, s], xrecv.at[q, s], partner)

    def wave_relay(q, s):
        slot = waves.at[from_pair(q) * nl + s]
        return remote(slot, slot, ysend.at[q, s], yrecv.at[q, s], partner)

    collect(gmsg, gin, gsend, grecv, 0)
    gram = mats[0]
    row_of = lax.broadcasted_iota(jnp.int32, (nvec, depth), 0)
    lane_of = lax.broadcasted_iota(jnp.int32, (nvec, depth), 1)
    inverse = jnp.where(row_of == lane_of, 1.0, 0.0)
    for k in range(nvec):
        scale = 1.0 / jnp.sqrt(gram[k : k + 1, k : k + 1])
        column = gram[:, k : k + 1] * scale
        line = inverse[k : k + 1] * scale
        inverse = jnp.where(row_of > k, inverse - column * line, jnp.where(row_of == k, line, inverse))
        gram = gram - column * (gram[k : k + 1] * scale)
    mats[1] = inverse
    own_rows = mats[1, pl.ds(me_v * nl, nl)]
    for i in range(nvec):
        coef[i] = jnp.broadcast_to(own_rows[:, i : i + 1], (nl, depth))

    def rotate(buffer, out, base, count, fresh):
        def one(row, carry):
            totals = [None if fresh else out[s, row] for s in range(nl)]
            for i in range(count):
                value = buffer[base + i, row]
                for s in range(nl):
                    term = coef[base + i, s : s + 1] * value
                    totals[s] = term if totals[s] is None else totals[s] + term
            for s in range(nl):
                out[s, row] = totals[s]
            return carry

        lax.fori_loop(0, rows, one, 0)

    rotate(held, rotated, 0, nvec, True)
    for s in range(nl):
        @pl.when(jnp.logical_not(own_slot(s)))
        def _():
            slot = waves.at[me_v * nl + s]
            remote(phi.at[0:rows], slot, bsend.at[0], brecv.at[s], partner).wait_recv()

        for q in range(1, pairs):
            wave_over(q, s).start()
        wave_core(s).start()
        if 2 * (s + 1) == nl:
            cmsg[: nl // 2] = products(waves, range(nl // 2))

    cmsg[nl // 2 :] = products(waves, range(nl // 2, nl))
    spread(cmsg, cin, csend, crecv)
    for q in range(1, pairs):
        for s in range(nl):
            wave_from(q, s).wait_recv()
            wave_relay(q, s).start()

    for s in range(nl):
        slot = waves.at[(pair * 2 + 1 - core) * nl + s]
        remote(slot, slot, psend.at[s], precv.at[s], partner).wait_recv()
    rotate(waves, potentials, pair * 2 * nl, 2 * nl, True)
    for q in range(1, pairs):
        for s in range(nl):
            wave_relay(q, s).wait_recv()
        rotate(waves, potentials, lax.rem(pair - q + pairs, pairs) * 2 * nl, 2 * nl, False)

    collect(cmsg, cin, csend, crecv, 2)
    cross = mats[2]
    high = lax.Precision.HIGHEST
    last_dims = (((1,), (1,)), ((), ()))
    inverse = mats[1]
    small = inverse[:, :nvec]
    middle = 0.5 * (
        jnp.dot(small, cross, precision=high)[:, :nvec]
        + lax.dot_general(inverse, cross, last_dims, precision=high)
    )
    ritz[...] = lax.dot_general(middle, small, last_dims, precision=high)

    for s in range(nl):
        @pl.when(jnp.logical_not(own_slot(s)))
        def _():
            forward(s).wait_send()

        wave_core(s).wait_send()
    for bx in range(blocks):
        @pl.when(jnp.logical_not(jnp.logical_and(bx * 2 + core == me_g, owner_v == me_v)))
        def _():
            back(bx).wait_send()
    for q in range(pairs):
        trial_copy(q).wait_send()
    for q in range(1, pairs):
        trial_relay(q).wait_send()
        for s in range(nl):
            wave_over(q, s).wait_send()
            wave_relay(q, s).wait_send()


def paired_body(trial_block, response_weight):
    nl, rows, cols, depth = trial_block.shape
    groups, parts = lax.axis_size("grid"), lax.axis_size("vec")
    nvec, blocks = parts * nl, groups // 2
    pairs, length, devices = parts // 2, (groups // 2) * rows, groups * parts
    f32 = jnp.float32
    dma = pltpu.SemaphoreType.DMA
    vmem = pl.BlockSpec(memory_space=pltpu.VMEM)
    field = pltpu.VMEM((length, cols, depth), f32)
    whole = pltpu.VMEM((nvec, rows, cols, depth), f32)
    inbox = pltpu.VMEM((groups, parts, nl, depth), f32)
    message = pltpu.VMEM((nl, depth), f32)
    small = pltpu.VMEM((ITERS, 2, 8, depth), f32)
    return pl.pallas_call(
        functools.partial(kernel, groups, parts),
        out_shape=(
            pltpu.VMEM(trial_block.shape, f32),
            pltpu.VMEM(trial_block.shape, f32),
            pltpu.VMEM((nvec, nvec), f32),
        ),
        in_specs=[pl.BlockSpec(memory_space=pl.ANY)] * 2,
        out_specs=(vmem, vmem, vmem),
        scratch_shapes=[
            pltpu.VMEM((rows, cols, depth), f32),
            pltpu.VMEM((nl, rows, cols, depth), f32),
            pltpu.VMEM((length, cols + 2 * PAD, depth), f32),
            field, field, field, field, small, small, whole, whole,
            message, inbox, message, inbox,
            pltpu.VMEM((3, nvec, depth), f32), pltpu.VMEM((nvec, nl, depth), f32),
            dma((nl,)), dma((blocks,)), dma((2, blocks)), dma((2, blocks)),
            dma((ITERS,)), dma((ITERS,)), dma((pairs,)), dma((pairs,)), dma((pairs,)), dma((pairs,)),
            dma((blocks,)), dma((nl,)), dma((nl,)), dma((nl,)),
            dma((pairs, nl)), dma((pairs, nl)), dma((pairs, nl)), dma((pairs, nl)),
            dma((devices,)), dma((devices,)), dma((devices,)), dma((devices,)), dma((2,)),
        ],
        compiler_params=pltpu.CompilerParams(collective_id=0, has_side_effects=True),
    )(trial_block, response_weight)


def chosen_body(trial_block, response_weight):
    nl, rows, cols, depth = trial_block.shape
    groups, parts = lax.axis_size("grid"), lax.axis_size("vec")
    fits = (
        max(groups // 16, 2) == 2 and groups == 2 * nl and parts % 2 == 0 and rows == HALO
        and cols % 8 == 0 and cols >= PAD and parts * nl <= depth
    )
    return (paired_body if fits else body)(trial_block, response_weight)


def solution(mesh):
    placed = (P("vec", "grid", None, None), P("grid", None, None))
    return jax.shard_map(
        chosen_body,
        mesh=mesh,
        in_specs=placed,
        out_specs=(P("vec", "grid", None, None), P("vec", "grid", None, None), P()),
        check_vma=False,
    )
```

profile of v0, /device:TPU:0, one launch (start us, length us, event | category | flops | bytes accessed | tf_op | source)
XLA Modules:
  0.0 49.2 jit_solution(15605118229534949595)
XLA Ops:
  0.6 46.5 %shard_map.49 = (f32[4,6,32,128]{3,2,1,0:T(8,128)S(1)}, f32[4,6,32,128]{3,2,1,0:T(8,128)S(1)}, f32[16,16]{1,0:T(8,128)S(1)}) custom-call(f32[4,6,32,128]{3,2,1,0:T(8,128)} %trial.1, f32[6,32,128]{2,1,0:T(8,128)} %weight.1), custom_call_target="tpu_custom_call" | custom-call | tf_op jit(solution)/shard_map/pallas_call | solution.py:527
  47.1 0.7 %copy.8 = f32[4,6,32,128]{3,2,1,0:T(8,128)} copy(f32[4,6,32,128]{3,2,1,0:T(8,128)S(1)} %get-tuple-element.3) | data formatting | bytes 786432
  47.9 0.6 %copy.10 = f32[16,16]{1,0:T(8,128)} copy(f32[16,16]{1,0:T(8,128)S(1)} %get-tuple-element.5) | data formatting | bytes 2048
  48.5 0.7 %copy.9 = f32[4,6,32,128]{3,2,1,0:T(8,128)} copy(f32[4,6,32,128]{3,2,1,0:T(8,128)S(1)} %get-tuple-element.4) | data formatting | bytes 786432
where the time goes:
time: 49.4 us; the launch traced here: 49.2 us
  Pallas kernels  46.5 us (94%)
  local copies, waits for them, and re-layouts  2.09 us (4%)
  between operations  0.64 us (1%)
    pallas_call x1, Pallas kernels, paired_body(): pl.pallas_call(functools.partial(kernel, groups, parts), out_shape=(pltpu...  46.5 us
    unnamed x3, local copies, waits for them, and re-layouts  2.09 us

commit v1 on v0

v1 whole, which is shorter than its diff:
```python
import functools

import jax
import jax.numpy as jnp
import numpy as np
from jax import lax
from jax.experimental import pallas as pl
from jax.experimental.pallas import tpu as pltpu
from jax.sharding import PartitionSpec as P

ITERS = 3


COEFFS = (
    -5369.0 / 1800.0,
    12.0 / 7.0,
    -15.0 / 56.0,
    10.0 / 189.0,
    -1.0 / 112.0,
    2.0 / 1925.0,
    -1.0 / 16632.0,
)


def shifted(value, axis, steps):
    count = lax.axis_size(axis)
    pairs = [(source, (source + steps) % count) for source in range(count)]
    return lax.ppermute(value, axis, pairs)


def with_halo(cells, sides, width):
    for axis, dim in sides:
        count = lax.axis_size(axis)
        head = lax.slice_in_dim(cells, 0, width, axis=dim)
        tail = lax.slice_in_dim(cells, cells.shape[dim] - width, cells.shape[dim], axis=dim)
        cells = jnp.concatenate(
            [
                lax.ppermute(tail, axis, [(i, (i + 1) % count) for i in range(count)]),
                cells,
                lax.ppermute(head, axis, [((i + 1) % count, i) for i in range(count)]),
            ],
            axis=dim,
        )
    return cells


def along_axis(total, padded, axis, length):
    for offset in range(1, 7):
        upper = lax.slice_in_dim(padded, 6 + offset, 6 + offset + length, axis=axis)
        lower = lax.slice_in_dim(padded, 6 - offset, 6 - offset + length, axis=axis)
        total = total + COEFFS[offset] * (upper + lower)
    return total


def operate(field):
    stride = max(lax.axis_size("grid") // 16, 2)
    row_count = field.shape[1]
    col_count = field.shape[2]
    total = 3.0 * COEFFS[0] * field
    below = shifted(field, "grid", stride)
    above = shifted(field, "grid", -stride)
    along_x = jnp.concatenate([below, field, above], axis=1)
    total = along_axis(total, along_x, 1, row_count)
    side_halo = with_halo(field, (("grid", 2),), 6)
    total = along_axis(total, side_halo, 2, col_count)
    along_z = jnp.pad(field, ((0, 0), (0, 0), (0, 0), (6, 6)))
    total = along_axis(total, along_z, 3, field.shape[3])
    return -total


def inner(left, right):
    return jnp.sum(left * right, axis=(1, 2, 3))


def expand(values):
    return values[:, None, None, None]


def two_products(residual, image):
    return lax.psum((inner(residual, residual), inner(residual, image)), "grid")


def finish(gram, cross, cells):
    high = lax.Precision.HIGHEST
    gram = gram / cells
    cross = cross / cells
    lower = jnp.linalg.cholesky(gram)
    inverse = lax.linalg.triangular_solve(
        lower, jnp.eye(gram.shape[0], dtype=jnp.float32), left_side=True, lower=True
    )
    middle = jnp.dot(inverse, 0.5 * (cross + cross.T), precision=high)
    return (inverse, jnp.dot(middle, inverse.T, precision=high))


def body(trial_block, response_weight):
    high = lax.Precision.HIGHEST
    source = response_weight[None] * trial_block
    solution = jnp.zeros_like(source)
    residual = source
    image = operate(residual)
    norm_now, product = two_products(residual, image)
    alpha = norm_now / product
    direction, along = (residual, image)
    for step in range(ITERS):
        solution = solution + expand(alpha) * direction
        residual = residual - expand(alpha) * along
        if step + 1 < ITERS:
            image = operate(residual)
            norm_next, product = two_products(residual, image)
            ratio = norm_next / norm_now
            alpha = norm_next / (product - ratio * norm_next / alpha)
            direction = residual + expand(ratio) * direction
            along = image + expand(ratio) * along
            norm_now = norm_next
    local_count = trial_block.shape[0]
    whole_x, whole_p = (
        lax.all_gather(trial_block, "vec", axis=0, tiled=True),
        lax.all_gather(solution, "vec", axis=0, tiled=True),
    )
    flat_x = whole_x.reshape(whole_x.shape[0], -1)
    flat_p = whole_p.reshape(whole_p.shape[0], -1)
    gram, cross = lax.psum(
        (jnp.dot(flat_x, flat_x.T, precision=high), jnp.dot(flat_x, flat_p.T, precision=high)),
        "grid",
    )
    cells = lax.axis_size("grid") * flat_x.shape[1]
    inverse, ritz_matrix = finish(gram, cross, cells)
    own_rows = lax.dynamic_slice_in_dim(
        inverse, lax.axis_index("vec") * local_count, local_count, 0
    )
    rotated = jnp.dot(own_rows, flat_x, precision=high).reshape(trial_block.shape)
    potentials = jnp.dot(own_rows, flat_p, precision=high).reshape(trial_block.shape)
    return (rotated, potentials, ritz_matrix)


MESH_ID = pl.DeviceIdType.MESH
PAD = 8
HALO = 6
ROUNDS = 4


def split_loss():
    exact = np.array(COEFFS[1:], np.float32)
    high = exact.astype(jnp.bfloat16).astype(np.float32)
    low = (exact - high).astype(jnp.bfloat16).astype(np.float32)
    return float(2.0 * np.sum(exact.astype(np.float64) - high - low))


CENTRE = 3.0 * COEFFS[0] + split_loss()


def kernel(
    groups, parts, trial, weight, rotated, potentials, ritz,
    wbuf, src, res, res1, res2, img, img1, phi, band, held, waves, gmsg, gin, cmsg, cin, mats, coef,
    near, fsend, frecv, tsend, trecv, rsend, rrecv, bsend, brecv, psend, precv, xsend, xrecv,
    ysend, yrecv, gsend, grecv, csend, crecv, isend,
):
    nl, rows, cols, depth = trial.shape
    nvec = parts * nl
    blocks = groups // 2
    mid = blocks // 2
    length = blocks * rows
    wide_y = 2 * cols
    total_devices = groups * parts
    f32, bf16 = jnp.float32, jnp.bfloat16
    me_g = lax.axis_index("grid")
    me_v = lax.axis_index("vec")
    me = me_g * parts + me_v
    z, y = lax.div(me_g, 2), lax.rem(me_g, 2)
    x, c = lax.div(me_v, 2), lax.rem(me_v, 2)
    center = slice(PAD, PAD + wide_y)

    def place(pz, py, px, pc):
        return (pz * 2 + py, px * 2 + pc)

    partner = place(z, y, x, 1 - c)
    barrier = pltpu.get_barrier_semaphore()

    def greet(sem, device):
        pl.semaphore_signal(sem, inc=1, device_id=device, device_id_type=MESH_ID)

    def around(sem, cores):
        for core in cores:
            greet(sem, place(z, y, 1 - x, core))
            greet(sem, place(z, 1 - y, x, core))

            @pl.when(z > 0)
            def _():
                greet(sem, place(z - 1, y, x, core))

            @pl.when(z < blocks - 1)
            def _():
                greet(sem, place(z + 1, y, x, core))

    sides = 4 - jnp.where(z > 0, 0, 1) - jnp.where(z < blocks - 1, 0, 1)
    greet(barrier, partner)
    around(barrier, (c, 1 - c))

    fetches = [
        pltpu.make_async_copy(weight, wbuf, isend.at[0]),
        pltpu.make_async_copy(trial, held.at[pl.ds(me_v * nl, nl)], isend.at[1]),
    ]
    for fetch in fetches:
        fetch.start()

    row_id = lax.broadcasted_iota(jnp.int32, (depth, depth), 0)
    gap = jnp.abs(row_id - lax.broadcasted_iota(jnp.int32, (depth, depth), 1))
    taps = jnp.zeros((depth, depth), f32)
    for k in range(1, HALO + 1):
        taps = jnp.where(gap == k, COEFFS[k], taps)
    taps_high = taps.astype(bf16)
    taps_low = (taps - taps_high.astype(f32)).astype(bf16)
    band[0:depth, 0:depth] = taps_high
    band[depth:, 0:depth] = taps_high
    band[0:depth, depth:] = taps_low
    band[depth:, depth:] = taps_low

    for fetch in fetches:
        fetch.wait()

    def prepare(i, carry):
        scale = wbuf[i]
        for s in range(nl):
            src[s, i] = scale * held[me_v * nl + s, i]
        return carry

    lax.fori_loop(0, rows, prepare, 0)
    pl.semaphore_wait(barrier, 1 + 2 * sides)

    def remote(source, target, send, recv, device):
        return pltpu.make_async_remote_copy(
            src_ref=source, dst_ref=target, send_sem=send, recv_sem=recv,
            device_id=device, device_id_type=MESH_ID,
        )

    def slab(bz, by):
        return res.at[pl.ds(bz * rows, rows), pl.ds(pl.multiple_of(PAD + by * cols, PAD), cols)]

    def host_of(s):
        return (mid - 1 + c, s % 2, x, s // 2)

    def own_slot(s):
        hz, hy, _, hc = host_of(s)
        return jnp.logical_and(jnp.logical_and(hz == z, hy == y), hc == c)

    def hops(s):
        hz, hy, _, _ = host_of(s)
        return jnp.abs(hz - z) + jnp.abs(hy - y)

    def forward(s):
        return remote(src.at[s], slab(z, y), fsend.at[s], frecv.at[me_g], place(*host_of(s)))

    def send_forward(s, test):
        @pl.when(jnp.logical_and(test, jnp.logical_not(own_slot(s))))
        def _():
            forward(s).start()

    def slot_ref(buffer, v):
        return buffer.at[pl.ds(v * nl, nl)]

    own_trial = slot_ref(held, me_v)
    trial_copies = [
        remote(own_trial, own_trial, tsend.at[0], trecv.at[0], partner),
        remote(own_trial, own_trial, tsend.at[1], trecv.at[1 + c], place(z, y, 1 - x, 0)),
    ]

    def trial_arrival(core):
        slot = slot_ref(held, (1 - x) * 2 + core)
        return remote(slot, slot, tsend.at[1], trecv.at[1 + core], partner)

    def trial_relay(core):
        slot = slot_ref(held, (1 - x) * 2 + core)
        return remote(slot, slot, rsend.at[core], rrecv.at[core], partner)

    around(near.at[0], (c,))
    for s in range(nl // 2):
        send_forward(s, hops(s) <= 1)
    trial_copies[1].start()
    trial_copies[0].start()
    for reach in range(2, ROUNDS + 2):
        pl.semaphore_wait(near.at[reach - 2], sides)
        if reach < ROUNDS + 1:
            around(near.at[reach - 1], (c,))
        if reach == 2:
            for s in range(nl // 2):
                send_forward(s, hops(s) == 2)
        if reach == 3:
            for s in range(nl // 2):
                send_forward(s, hops(s) > 2)
            for s in range(nl // 2, nl):
                send_forward(s, hops(s) >= 0)

    for s in range(nl):
        @pl.when(own_slot(s))
        def _():
            res[pl.ds(z * rows, rows), pl.ds(pl.multiple_of(PAD + y * cols, PAD), cols)] = src[s]

    hosted_c = z - (mid - 1)
    hosted_s = c * 2 + y
    hosted_v = x * 2 + hosted_c
    hosts = jnp.logical_and(z >= mid - 1, z <= mid)

    def along_depth(value):
        high = value.astype(bf16)
        low = (value - high.astype(f32)).astype(bf16)
        both = jnp.dot(
            jnp.concatenate([high, low], axis=1), band[...], preferred_element_type=f32
        )
        return both[:, :depth] + both[:, depth:]

    def folded(value):
        return value.reshape(wide_y // 8, 8, depth).sum(axis=0)

    def full(value):
        return jnp.sum(value, axis=(0, 1), keepdims=True)

    def wide(value):
        return jnp.broadcast_to(value, (wide_y, depth))

    def sweep(one, start):
        return lax.fori_loop(0, length, one, start, unroll=length)

    zero = jnp.zeros((8, depth), f32)

    def wrap(field, i, value):
        field[lax.rem(i + rows, length), 0:PAD] = value[wide_y - PAD :]
        field[lax.rem(i + length - rows, length), PAD + wide_y :] = value[:PAD]

    def operate(field, image):
        def one(i, carry):
            norm, product = carry
            value = field[i, center]
            acc = CENTRE * value + along_depth(value)
            for k in range(1, HALO + 1):
                beside = field[lax.rem(i + k, length), center]
                beside = beside + field[lax.rem(i + length - k, length), center]
                across = field[i, PAD + k : PAD + k + wide_y] + field[i, PAD - k : PAD - k + wide_y]
                acc = acc + COEFFS[k] * (beside + across)
            acc = -acc
            image[i] = acc
            return (norm + folded(value * value), product + folded(value * acc))

        norm, product = sweep(one, (zero, zero))
        return full(norm), full(product)

    def energy(field):
        def one(i, carry):
            norm, product = carry
            value = field[i, center]
            acc = (0.5 * CENTRE) * value + 0.5 * along_depth(value)
            for k in range(1, HALO + 1):
                ahead = field[lax.rem(i + k, length), center]
                acc = acc + COEFFS[k] * (ahead + field[i, PAD + k : PAD + k + wide_y])
            return (norm + folded(value * value), product + folded(value * acc))

        norm, product = sweep(one, (zero, zero))
        return full(norm), -2.0 * full(product)

    def back(order, by):
        bz = order + hosted_c * (blocks - 1 - 2 * order)
        return bz, remote(
            phi.at[pl.ds(bz * rows, rows), by * cols : (by + 1) * cols],
            waves.at[hosted_v * nl + hosted_s],
            bsend.at[order * 2 + by], brecv.at[hosted_s], place(bz, by, x, hosted_c),
        )

    def kept(bz, by):
        return jnp.logical_and(jnp.logical_and(bz == z, by == y), hosted_c == c)

    orders = list(range(blocks - 1, mid - 1, -1)) + list(range(mid))

    @pl.when(hosts)
    def _():
        for bg in range(groups):
            @pl.when(jnp.logical_not(jnp.logical_and(bg == me_g, hosted_c == c)))
            def _():
                remote(
                    src.at[0], slab(bg // 2, bg % 2), fsend.at[0], frecv.at[bg], partner
                ).wait_recv()

        def fill(i, carry):
            field = res
            field[lax.rem(i + rows, length), 0:PAD] = field[i, wide_y : wide_y + PAD]
            field[lax.rem(i + length - rows, length), PAD + wide_y :] = field[i, PAD : 2 * PAD]
            return carry

        sweep(fill, 0)
        norm, product = operate(res, img)
        alpha = norm / product
        alpha_wide = wide(alpha)

        def first(i, carry):
            value = res[i, center] - alpha_wide * img[i]
            res1[i, center] = value
            wrap(res1, i, value)
            return carry

        sweep(first, 0)
        norm1, product = operate(res1, img1)
        ratio1 = norm1 / norm
        alpha1 = norm1 / (product - ratio1 * norm1 / alpha)
        image1_wide, image0_wide = wide(alpha1), wide(alpha1 * ratio1)

        def second(i, carry):
            value = res1[i, center] - image1_wide * img1[i] - image0_wide * img[i]
            res2[i, center] = value
            wrap(res2, i, value)
            return carry

        sweep(second, 0)
        norm2, product = energy(res2)
        ratio2 = norm2 / norm1
        alpha2 = norm2 / (product - ratio2 * norm2 / alpha1)
        share1 = alpha1 + alpha2 * ratio2
        share0 = wide(alpha + share1 * ratio1)
        share1 = wide(share1)
        share2 = wide(alpha2)
        for order in orders:
            bz = order + hosted_c * (blocks - 1 - 2 * order)

            def last(i, carry):
                row = bz * rows + i
                phi[row] = (
                    share0 * res[row, center] + share1 * res1[row, center] + share2 * res2[row, center]
                )
                return carry

            lax.fori_loop(0, rows, last, 0, unroll=rows)
            for by in range(2):
                _, copy = back(order, by)

                @pl.when(jnp.logical_not(kept(bz, by)))
                def _():
                    copy.start()

                @pl.when(kept(bz, by))
                def _():
                    waves[hosted_v * nl + hosted_s] = phi[
                        pl.ds(bz * rows, rows), by * cols : (by + 1) * cols
                    ]

    def products(buffer, base, slots):
        lane_row = lax.broadcasted_iota(jnp.int32, (len(slots), depth), 1)

        def one(j, acc):
            other = held[j]
            parts_of = [
                jnp.sum(jnp.sum(buffer[base + s] * other, axis=0), axis=0, keepdims=True)
                for s in slots
            ]
            value = jnp.sum(jnp.concatenate(parts_of, axis=0), axis=1, keepdims=True)
            return jnp.where(lane_row == j, value, acc)

        return lax.fori_loop(0, nvec, one, jnp.zeros((len(slots), depth), f32), unroll=4)

    def device_at(k):
        target = lax.rem(me + k, total_devices)
        return (lax.div(target, parts), lax.rem(target, parts))

    def spread(message, slot, send, recv):
        def start(k, carry):
            remote(message, slot, send.at[k], recv, device_at(k)).start()
            return carry

        lax.fori_loop(1, total_devices, start, 0)

    def drain(message, slot, send, recv):
        def wait(k, carry):
            remote(message, slot, send.at[k], recv, device_at(k)).wait_send()
            return carry

        lax.fori_loop(1, total_devices, wait, 0)

    gram_slot, gram_recv = gin.at[me_g * 2 + x], grecv.at[me_g * 2 + x]

    trial_copies[0].wait_recv()

    @pl.when(c == 0)
    def _():
        for core in range(2):
            trial_arrival(core).wait_recv()
            trial_relay(core).start()
        gmsg[...] = products(held, x * 2 * nl, range(2 * nl))
        gin[me_g * 2 + x] = gmsg[...]
        spread(gmsg, gram_slot, gsend, gram_recv)

    @pl.when(c == 1)
    def _():
        for core in range(2):
            trial_relay(core).wait_recv()

    def wave_over(s):
        slot = waves.at[me_v * nl + s]
        return remote(slot, slot, xsend.at[s], xrecv.at[s], place(z, y, 1, c))

    def wave_core(s):
        slot = waves.at[me_v * nl + s]
        return remote(slot, slot, psend.at[s], precv.at[s], partner)

    def wave_relay(s):
        slot = waves.at[c * nl + s]
        return remote(slot, slot, ysend.at[s], yrecv.at[s], partner)

    def take(s):
        @pl.when(jnp.logical_not(own_slot(s)))
        def _():
            slot = waves.at[me_v * nl + s]
            remote(slot, slot, bsend.at[0], brecv.at[s], partner).wait_recv()

        @pl.when(x == 0)
        def _():
            wave_over(s).start()

        @pl.when(c == 0)
        def _():
            wave_core(s).start()

    def pass_on(s):
        slot = waves.at[c * nl + s]
        remote(slot, slot, xsend.at[s], xrecv.at[s], partner).wait_recv()
        wave_relay(s).start()

    first_half, last_half = range(nl // 2), range(nl // 2, nl)
    for s in first_half:
        take(s)
    cmsg[: nl // 2] = products(waves, me_v * nl, first_half)

    def gather_gram(i, carry):
        owner = lax.rem(i, 2) * 2 + lax.div(i, 2) * parts

        @pl.when(owner != me)
        def _():
            remote(gmsg, gin.at[i], gsend.at[0], grecv.at[i], partner).wait_recv()

        return carry

    lax.fori_loop(0, groups * 2, gather_gram, 0)
    cells = groups * rows * cols * depth
    for px in range(2):
        total = gin[px]
        for g in range(1, groups):
            total = total + gin[g * 2 + px]
        mats[0, px * 2 * nl : (px + 1) * 2 * nl] = total / cells
    gram = mats[0]
    row_of = lax.broadcasted_iota(jnp.int32, (nvec, depth), 0)
    lane_of = lax.broadcasted_iota(jnp.int32, (nvec, depth), 1)
    inverse = jnp.where(row_of == lane_of, 1.0, 0.0)
    for k in range(nvec):
        scale = 1.0 / jnp.sqrt(gram[k : k + 1, k : k + 1])
        column = gram[:, k : k + 1] * scale
        line = inverse[k : k + 1] * scale
        inverse = jnp.where(row_of > k, inverse - column * line, jnp.where(row_of == k, line, inverse))
        gram = gram - column * (gram[k : k + 1] * scale)
    mats[1] = inverse
    own_rows = mats[1, pl.ds(me_v * nl, nl)]
    for i in range(nvec):
        coef[i] = jnp.broadcast_to(own_rows[:, i : i + 1], (nl, depth))

    def rotate(buffer, out, base, count, fresh):
        def one(row, carry):
            totals = [None if fresh else out[s, row] for s in range(nl)]
            for i in range(count):
                value = buffer[base + i, row]
                for s in range(nl):
                    term = coef[base + i, s : s + 1] * value
                    totals[s] = term if totals[s] is None else totals[s] + term
            for s in range(nl):
                out[s, row] = totals[s]
            return carry

        lax.fori_loop(0, rows, one, 0)

    rotate(held, rotated, 0, nvec, True)

    @pl.when(x == 1)
    def _():
        for s in first_half:
            pass_on(s)

    for s in last_half:
        take(s)
    cmsg[nl // 2 :] = products(waves, me_v * nl, last_half)
    cin[me] = cmsg[...]
    cross_slot, cross_recv = cin.at[me], crecv.at[me]
    spread(cmsg, cross_slot, csend, cross_recv)
    rotate(waves, potentials, me_v * nl, nl, True)

    @pl.when(x == 1)
    def _():
        for s in last_half:
            pass_on(s)

    @pl.when(c == 1)
    def _():
        for s in range(nl):
            slot = waves.at[x * 2 * nl + s]
            remote(slot, slot, psend.at[s], precv.at[s], partner).wait_recv()
        rotate(waves, potentials, x * 2 * nl, nl, False)

    @pl.when(x == 1)
    def _():
        rotate(waves, potentials, c * nl, nl, False)
        for s in range(nl):
            slot = waves.at[(1 - c) * nl + s]
            remote(slot, slot, ysend.at[s], yrecv.at[s], partner).wait_recv()
        rotate(waves, potentials, (1 - c) * nl, nl, False)

    def gather_cross(i, carry):
        @pl.when(i != me)
        def _():
            remote(cmsg, cin.at[i], csend.at[0], crecv.at[i], partner).wait_recv()

        return carry

    lax.fori_loop(0, total_devices, gather_cross, 0)
    for v in range(parts):
        total = cin[v]
        for g in range(1, groups):
            total = total + cin[g * parts + v]
        mats[2, v * nl : (v + 1) * nl] = total / cells
    cross = mats[2]
    high = lax.Precision.HIGHEST
    last_dims = (((1,), (1,)), ((), ()))
    inverse = mats[1]
    small = inverse[:, :nvec]
    middle = 0.5 * (
        jnp.dot(small, cross, precision=high)[:, :nvec]
        + lax.dot_general(inverse, cross, last_dims, precision=high)
    )
    ritz[...] = lax.dot_general(middle, small, last_dims, precision=high)

    for s in range(nl):
        @pl.when(jnp.logical_not(own_slot(s)))
        def _():
            forward(s).wait_send()

        @pl.when(x == 0)
        def _():
            wave_over(s).wait_send()

        @pl.when(c == 0)
        def _():
            wave_core(s).wait_send()

        @pl.when(x == 1)
        def _():
            wave_relay(s).wait_send()

    @pl.when(hosts)
    def _():
        for order in orders:
            for by in range(2):
                bz, copy = back(order, by)

                @pl.when(jnp.logical_not(kept(bz, by)))
                def _():
                    copy.wait_send()

    for copy in trial_copies:
        copy.wait_send()

    @pl.when(c == 0)
    def _():
        for core in range(2):
            trial_relay(core).wait_send()
        drain(gmsg, gram_slot, gsend, gram_recv)

    drain(cmsg, cross_slot, csend, cross_recv)


def hosted_body(trial_block, response_weight):
    nl, rows, cols, depth = trial_block.shape
    groups, parts = lax.axis_size("grid"), lax.axis_size("vec")
    nvec, blocks = parts * nl, groups // 2
    length, wide_y, devices = blocks * rows, 2 * cols, groups * parts
    f32 = jnp.float32
    dma = pltpu.SemaphoreType.DMA
    vmem = pl.BlockSpec(memory_space=pltpu.VMEM)
    field = pltpu.VMEM((length, wide_y, depth), f32)
    padded = pltpu.VMEM((length, wide_y + 2 * PAD, depth), f32)
    whole = pltpu.VMEM((nvec, rows, cols, depth), f32)
    return pl.pallas_call(
        functools.partial(kernel, groups, parts),
        out_shape=(
            pltpu.VMEM(trial_block.shape, f32),
            pltpu.VMEM(trial_block.shape, f32),
            pltpu.VMEM((nvec, nvec), f32),
        ),
        in_specs=[pl.BlockSpec(memory_space=pl.ANY)] * 2,
        out_specs=(vmem, vmem, vmem),
        scratch_shapes=[
            pltpu.VMEM((rows, cols, depth), f32),
            pltpu.VMEM((nl, rows, cols, depth), f32),
            padded, padded, padded, field, field, field,
            pltpu.VMEM((2 * depth, 2 * depth), jnp.bfloat16), whole, whole,
            pltpu.VMEM((2 * nl, depth), f32), pltpu.VMEM((2 * groups, 2 * nl, depth), f32),
            pltpu.VMEM((nl, depth), f32), pltpu.VMEM((devices, nl, depth), f32),
            pltpu.VMEM((3, nvec, depth), f32), pltpu.VMEM((nvec, nl, depth), f32),
            pltpu.SemaphoreType.REGULAR((ROUNDS,)),
            dma((nl,)), dma((groups,)), dma((2,)), dma((3,)), dma((2,)), dma((2,)),
            dma((groups,)), dma((nl,)), dma((nl,)), dma((nl,)), dma((nl,)), dma((nl,)),
            dma((nl,)), dma((nl,)),
            dma((devices,)), dma((2 * groups,)), dma((devices,)), dma((devices,)), dma((2,)),
        ],
        compiler_params=pltpu.CompilerParams(collective_id=0, has_side_effects=True),
    )(trial_block, response_weight)


def chosen_body(trial_block, response_weight):
    nl, rows, cols, depth = trial_block.shape
    groups, parts = lax.axis_size("grid"), lax.axis_size("vec")
    fits = (
        max(groups // 16, 2) == 2 and groups == 2 * nl and parts == nl and groups == 2 * ROUNDS
        and rows == HALO and cols % 8 == 0 and cols >= PAD and parts * nl <= depth
    )
    return (hosted_body if fits else body)(trial_block, response_weight)


def solution(mesh):
    placed = (P("vec", "grid", None, None), P("grid", None, None))
    return jax.shard_map(
        chosen_body,
        mesh=mesh,
        in_specs=placed,
        out_specs=(P("vec", "grid", None, None), P("vec", "grid", None, None), P()),
        check_vma=False,
    )
```

time: 49.4 us -> 44.2 us (0.89)
  Pallas kernels: 46.5 us -> 41.3 us
    pallas_call x1, Pallas kernels: 46.5 us -> 41.3 us  [hosted_body(): pl.pallas_call(functools.partial(kernel, groups, parts), out_shape=(pltpu...]
where the time goes in v1:
time: 44.2 us; the launch traced here: 44.1 us
  Pallas kernels  41.3 us (93%)
  local copies, waits for them, and re-layouts  2.09 us (5%)
  between operations  0.64 us (1%)
    pallas_call x1, Pallas kernels, hosted_body(): pl.pallas_call(functools.partial(kernel, groups, parts), out_shape=(pltpu...  41.3 us
    unnamed x3, local copies, waits for them, and re-layouts  2.09 us

profile of v1, /device:TPU:0, one launch (start us, length us, event | category | flops | bytes accessed | tf_op | source)
XLA Modules:
  0.0 44.1 jit_solution(13426873125026220846)
XLA Ops:
  0.6 41.3 %shard_map.49 = (f32[4,6,32,128]{3,2,1,0:T(8,128)S(1)}, f32[4,6,32,128]{3,2,1,0:T(8,128)S(1)}, f32[16,16]{1,0:T(8,128)S(1)}) custom-call(f32[4,6,32,128]{3,2,1,0:T(8,128)} %trial.1, f32[6,32,128]{2,1,0:T(8,128)} %weight.1), custom_call_target="tpu_custom_call" | custom-call | tf_op jit(solution)/shard_map/pallas_call | solution.py:682
  42.0 0.7 %copy.8 = f32[4,6,32,128]{3,2,1,0:T(8,128)} copy(f32[4,6,32,128]{3,2,1,0:T(8,128)S(1)} %get-tuple-element.3) | data formatting | bytes 786432
  42.7 0.6 %copy.10 = f32[16,16]{1,0:T(8,128)} copy(f32[16,16]{1,0:T(8,128)S(1)} %get-tuple-element.5) | data formatting | bytes 2048
  43.3 0.7 %copy.9 = f32[4,6,32,128]{3,2,1,0:T(8,128)} copy(f32[4,6,32,128]{3,2,1,0:T(8,128)S(1)} %get-tuple-element.4) | data formatting | bytes 786432

commit v2 on v1

--- a/solution.py
+++ b/solution.py
@@ -136,7 +136,6 @@
 MESH_ID = pl.DeviceIdType.MESH
 PAD = 8
 HALO = 6
-ROUNDS = 4
 
 
 def split_loss():
@@ -179,22 +178,21 @@
     def greet(sem, device):
         pl.semaphore_signal(sem, inc=1, device_id=device, device_id_type=MESH_ID)
 
-    def around(sem, cores):
-        for core in cores:
-            greet(sem, place(z, y, 1 - x, core))
-            greet(sem, place(z, 1 - y, x, core))
-
-            @pl.when(z > 0)
+    within = 0
+    for step in range(1, groups):
+        for core in range(2):
+            there = lax.rem(me_g + step, groups)
+            far = jnp.abs(lax.div(there, 2) - z) + jnp.abs(lax.rem(there, 2) - y) > 3
+            within = within + jnp.where(far, 0, 1)
+
+            @pl.when(jnp.logical_not(far))
             def _():
-                greet(sem, place(z - 1, y, x, core))
-
-            @pl.when(z < blocks - 1)
-            def _():
-                greet(sem, place(z + 1, y, x, core))
-
-    sides = 4 - jnp.where(z > 0, 0, 1) - jnp.where(z < blocks - 1, 0, 1)
+                greet(barrier, (there, x * 2 + core))
+
     greet(barrier, partner)
-    around(barrier, (c, 1 - c))
+    for core in range(2):
+        greet(barrier, place(z, y, 1 - x, core))
+    greet(barrier, place(z, 1 - y, 1 - x, c))
 
     fetches = [
         pltpu.make_async_copy(weight, wbuf, isend.at[0]),
@@ -225,7 +223,7 @@
         return carry
 
     lax.fori_loop(0, rows, prepare, 0)
-    pl.semaphore_wait(barrier, 1 + 2 * sides)
+    pl.semaphore_wait(barrier, within + 4)
 
     def remote(source, target, send, recv, device):
         return pltpu.make_async_remote_copy(
@@ -243,15 +241,11 @@
         hz, hy, _, hc = host_of(s)
         return jnp.logical_and(jnp.logical_and(hz == z, hy == y), hc == c)
 
-    def hops(s):
-        hz, hy, _, _ = host_of(s)
-        return jnp.abs(hz - z) + jnp.abs(hy - y)
-
     def forward(s):
         return remote(src.at[s], slab(z, y), fsend.at[s], frecv.at[me_g], place(*host_of(s)))
 
-    def send_forward(s, test):
-        @pl.when(jnp.logical_and(test, jnp.logical_not(own_slot(s))))
+    def send_forward(s):
+        @pl.when(jnp.logical_not(own_slot(s)))
         def _():
             forward(s).start()
 
@@ -272,28 +266,18 @@
         slot = slot_ref(held, (1 - x) * 2 + core)
         return remote(slot, slot, rsend.at[core], rrecv.at[core], partner)
 
-    around(near.at[0], (c,))
-    for s in range(nl // 2):
-        send_forward(s, hops(s) <= 1)
+    for s in range(nl):
+        send_forward(s)
     trial_copies[1].start()
     trial_copies[0].start()
-    for reach in range(2, ROUNDS + 2):
-        pl.semaphore_wait(near.at[reach - 2], sides)
-        if reach < ROUNDS + 1:
-            around(near.at[reach - 1], (c,))
-        if reach == 2:
-            for s in range(nl // 2):
-                send_forward(s, hops(s) == 2)
-        if reach == 3:
-            for s in range(nl // 2):
-                send_forward(s, hops(s) > 2)
-            for s in range(nl // 2, nl):
-                send_forward(s, hops(s) >= 0)
-
+    for device in (place(z, 1 - y, x, c), place(z, y, 1 - x, c), place(z, 1 - y, 1 - x, c)):
+        greet(near.at[0], device)
     for s in range(nl):
         @pl.when(own_slot(s))
         def _():
             res[pl.ds(z * rows, rows), pl.ds(pl.multiple_of(PAD + y * cols, PAD), cols)] = src[s]
+
+    pl.semaphore_wait(near.at[0], 3)
 
     hosted_c = z - (mid - 1)
     hosted_s = c * 2 + y
@@ -524,6 +508,18 @@
     for s in first_half:
         take(s)
     cmsg[: nl // 2] = products(waves, me_v * nl, first_half)
+
+    @pl.when(x == 1)
+    def _():
+        for s in first_half:
+            pass_on(s)
+
+    for s in last_half:
+        take(s)
+    cmsg[nl // 2 :] = products(waves, me_v * nl, last_half)
+    cin[me] = cmsg[...]
+    cross_slot, cross_recv = cin.at[me], crecv.at[me]
+    spread(cmsg, cross_slot, csend, cross_recv)
 
     def gather_gram(i, carry):
         owner = lax.rem(i, 2) * 2 + lax.div(i, 2) * parts
@@ -570,25 +566,14 @@
 
         lax.fori_loop(0, rows, one, 0)
 
-    rotate(held, rotated, 0, nvec, True)
-
-    @pl.when(x == 1)
-    def _():
-        for s in first_half:
-            pass_on(s)
-
-    for s in last_half:
-        take(s)
-    cmsg[nl // 2 :] = products(waves, me_v * nl, last_half)
-    cin[me] = cmsg[...]
-    cross_slot, cross_recv = cin.at[me], crecv.at[me]
-    spread(cmsg, cross_slot, csend, cross_recv)
     rotate(waves, potentials, me_v * nl, nl, True)
 
     @pl.when(x == 1)
     def _():
         for s in last_half:
             pass_on(s)
+
+    rotate(held, rotated, 0, nvec, True)
 
     @pl.when(c == 1)
     def _():
@@ -668,6 +653,18 @@
     drain(cmsg, cross_slot, csend, cross_recv)
 
 
+def place_results(*refs):
+    sources, targets, sems = refs[:3], refs[3:6], refs[6]
+    copies = [
+        pltpu.make_async_copy(source, target, sems.at[i])
+        for i, (source, target) in enumerate(zip(sources, targets))
+    ]
+    for copy in copies:
+        copy.start()
+    for copy in copies:
+        copy.wait()
+
+
 def hosted_body(trial_block, response_weight):
     nl, rows, cols, depth = trial_block.shape
     groups, parts = lax.axis_size("grid"), lax.axis_size("vec")
@@ -679,7 +676,7 @@
     field = pltpu.VMEM((length, wide_y, depth), f32)
     padded = pltpu.VMEM((length, wide_y + 2 * PAD, depth), f32)
     whole = pltpu.VMEM((nvec, rows, cols, depth), f32)
-    return pl.pallas_call(
+    results = pl.pallas_call(
         functools.partial(kernel, groups, parts),
         out_shape=(
             pltpu.VMEM(trial_block.shape, f32),
@@ -696,7 +693,7 @@
             pltpu.VMEM((2 * nl, depth), f32), pltpu.VMEM((2 * groups, 2 * nl, depth), f32),
             pltpu.VMEM((nl, depth), f32), pltpu.VMEM((devices, nl, depth), f32),
             pltpu.VMEM((3, nvec, depth), f32), pltpu.VMEM((nvec, nl, depth), f32),
-            pltpu.SemaphoreType.REGULAR((ROUNDS,)),
+            pltpu.SemaphoreType.REGULAR((1,)),
             dma((nl,)), dma((groups,)), dma((2,)), dma((3,)), dma((2,)), dma((2,)),
             dma((groups,)), dma((nl,)), dma((nl,)), dma((nl,)), dma((nl,)), dma((nl,)),
             dma((nl,)), dma((nl,)),
@@ -704,13 +701,20 @@
         ],
         compiler_params=pltpu.CompilerParams(collective_id=0, has_side_effects=True),
     )(trial_block, response_weight)
+    return pl.pallas_call(
+        place_results,
+        out_shape=tuple(jax.ShapeDtypeStruct(part.shape, f32) for part in results),
+        in_specs=[vmem] * 3,
+        out_specs=(pl.BlockSpec(memory_space=pl.ANY),) * 3,
+        scratch_shapes=[dma((3,))],
+    )(*(pltpu.with_memory_space_constraint(part, pltpu.VMEM) for part in results))
 
 
 def chosen_body(trial_block, response_weight):
     nl, rows, cols, depth = trial_block.shape
     groups, parts = lax.axis_size("grid"), lax.axis_size("vec")
     fits = (
-        max(groups // 16, 2) == 2 and groups == 2 * nl and parts == nl and groups == 2 * ROUNDS
+        max(groups // 16, 2) == 2 and groups == 2 * nl and parts == nl
         and rows == HALO and cols % 8 == 0 and cols >= PAD and parts * nl <= depth
     )
     return (hosted_body if fits else body)(trial_block, response_weight)

time: 44.2 us -> 41.3 us (0.934)
  local copies, waits for them, and re-layouts: 2.09 us -> 0 us
  Pallas kernels: 41.3 us -> 40.5 us
    unnamed x3 -> x0, local copies, waits for them, and re-layouts: 2.09 us -> none
    pallas_call x1, Pallas kernels: 41.3 us -> 39.6 us  [hosted_body(): pl.pallas_call(functools.partial(kernel, groups, parts), out_shape=(pltpu...]
    pallas_call x0 -> x1, Pallas kernels: none -> 0.91 us  [hosted_body(): pl.pallas_call(place_results, out_shape=tuple((jax.ShapeDtypeStruct(part....]
where the time goes in v2:
time: 41.3 us; the launch traced here: 41.1 us
  Pallas kernels  40.5 us (98%)
  between operations  0.64 us (2%)
    pallas_call x1, Pallas kernels, hosted_body(): pl.pallas_call(functools.partial(kernel, groups, parts), out_shape=(pltpu...  39.6 us
    pallas_call x1, Pallas kernels, hosted_body(): pl.pallas_call(place_results, out_shape=tuple((jax.ShapeDtypeStruct(part....  0.91 us

profile of v2, /device:TPU:0, one launch (start us, length us, event | category | flops | bytes accessed | tf_op | source)
XLA Modules:
  0.0 41.1 jit_solution(10721968074226767545)
XLA Ops:
  0.6 39.6 %shard_map.49 = (f32[4,6,32,128]{3,2,1,0:T(8,128)S(1)}, f32[4,6,32,128]{3,2,1,0:T(8,128)S(1)}, f32[16,16]{1,0:T(8,128)S(1)}) custom-call(f32[4,6,32,128]{3,2,1,0:T(8,128)} %trial.1, f32[6,32,128]{2,1,0:T(8,128)} %weight.1), custom_call_target="tpu_custom_call" | custom-call | tf_op jit(solution)/shard_map/pallas_call | solution.py:679
  40.2 0.9 %shard_map.50 = (f32[4,6,32,128]{3,2,1,0:T(8,128)}, f32[4,6,32,128]{3,2,1,0:T(8,128)}, f32[16,16]{1,0:T(8,128)}) custom-call(f32[4,6,32,128]{3,2,1,0:T(8,128)S(1)} %get-tuple-element.6.refs_0_, f32[4,6,32,128]{3,2,1,0:T(8,128)S(1)} %get-tuple-element.7.refs_1_, f32[16,16]{1,0:T(8,128)S(1)} %get-tuple-element.8.refs_2_), custom_call_target="tpu_custom_call" | custom-call | tf_op jit(solution)/shard_map/pallas_call | solution.py:704
